TPU v7x, 32 devices: a whole 2x2x4 slice. The times are simulated.
32 devices in a mesh: groups: 2 (over x), space: 16 (over z, y, core).
Axes of the slice: x: 2, y: 2, z: 4, core: 2. Of those that a mesh axis runs over, the one named last changes fastest.
Arguments:
- eigvecs: bfloat16 [32, 64, 2, 3, 128], P('groups', 'space'), parts along dimension 0, may hold values from -1.3515625 to 1.3515625
- phase_index: int32 [128], P('groups'), parts along dimension 0, may hold values from 0 to 47
- perambulator: bfloat16 [512, 2, 128, 128], P(('groups', 'space')), parts along dimension 0, may hold values from -0.046875 to 0.046875
- tile_sink: int32 [512, 1], P(('groups', 'space')), parts along dimension 0, may hold values from 0 to 15; in each aligned block of 16 rows (0 to 15, 16 to 31, ...) at most 2 rows name the same one
- tile_sep: int32 [512], P(('groups', 'space')), parts along dimension 0, may hold values from 0 to 7
- tile_diagram: int32 [512], P(('groups', 'space')), parts along dimension 0, may hold values from 0 to 1
Outputs:
- elementals: bfloat16 [32, 2, 128, 128], P(('groups', 'space')), parts along dimension 0
- correlator: float32 [512, 2], P(('groups', 'space')), parts along dimension 0
There are 2 independent parts, one for each index of `groups`. A program takes and returns all parts, laid end to end along the dimension named above; each array names one. Nothing has to cross between parts.
Inputs may be any that keep to these rules, and one draw needn't show every extreme that they name: `tile_sink`: in the tiles of one device no sink time is named by more than 2 tiles.
All inputs are finite; a program needn't handle non-finite values.
Results may differ from a plain program's by a relative error of at most 0.0048.
Values may be sent and summed in bfloat16 or wider, within the bound.
A program may use at most 128 MiB of HBM per device.

v0:
```python
import math
import jax
import jax.numpy as jnp
from jax import lax
from jax.sharding import PartitionSpec as P

PERIOD = 48


def make_right(vecs, cosine, sine):
    real_part = vecs[..., 0, :, :].astype(jnp.float32)
    imag_part = vecs[..., 1, :, :].astype(jnp.float32)
    cos_col = cosine[:, None, None]
    sin_col = sine[:, None, None]
    first = (cos_col * real_part - sin_col * imag_part).astype(jnp.bfloat16)
    second = (sin_col * real_part + cos_col * imag_part).astype(jnp.bfloat16)
    top = jnp.stack([first, second], -2)
    bottom = jnp.stack([second, -first], -2)
    return jnp.stack([top, bottom], -4)


def phases(indices):
    angle = 2.0 * math.pi / PERIOD * indices.astype(jnp.float32)
    return (jnp.cos(angle), jnp.sin(angle))


def contract_tiles(sink_mat, source_mat, tiles, diagram):

    def mult(left, right):
        return jnp.einsum("bij,bjk->bik", left, right, preferred_element_type=jnp.float32)

    tile_re = tiles[:, 0]
    tile_im = tiles[:, 1]
    trans_re = jnp.swapaxes(tile_re, 1, 2)
    trans_im = -jnp.swapaxes(tile_im, 1, 2)
    flag = (diagram == 1)[:, None, None]
    left_re = jnp.where(flag, trans_re, tile_re)
    left_im = jnp.where(flag, trans_im, tile_im)
    right_re = jnp.where(flag, tile_re, trans_re)
    right_im = jnp.where(flag, tile_im, trans_im)
    sink_re = sink_mat[:, 0]
    sink_im = sink_mat[:, 1]
    src_re = jnp.swapaxes(source_mat[:, 0], 1, 2)
    src_im = -jnp.swapaxes(source_mat[:, 1], 1, 2)
    first_re = mult(sink_re, left_re) - mult(sink_im, left_im)
    first_im = mult(sink_re, left_im) + mult(sink_im, left_re)
    second_re = jnp.swapaxes(mult(src_re, right_re) - mult(src_im, right_im), 1, 2)
    second_im = jnp.swapaxes(mult(src_re, right_im) + mult(src_im, right_re), 1, 2)
    trace_re = jnp.sum(first_re * second_re - first_im * second_im, axis=(1, 2))
    trace_im = jnp.sum(first_re * second_im + first_im * second_re, axis=(1, 2))
    return jnp.stack([trace_re, trace_im], -1)


def run_blocks(step_fn, items, total):
    block = math.gcd(32, total)
    shaped = tuple((item.reshape((total // block, block) + item.shape[1:]) for item in items))
    result = lax.map(step_fn, shaped)
    return result.reshape((total,) + result.shape[2:])


def local(eigvecs, phase_index, perambulator, tile_sink, tile_sep, tile_diagram):
    tile_count = perambulator.shape[0]
    sinks = tile_sink[:, 0]
    cosine, sine = phases(phase_index)
    slices = lax.all_to_all(eigvecs, "space", split_axis=0, concat_axis=1, tiled=True)
    vecs = slices[0]
    right = make_right(vecs, cosine, sine)
    value = jnp.einsum("spck,spcol->okl", vecs, right, preferred_element_type=jnp.float32)
    elemental = value.astype(jnp.bfloat16)[None]
    gathered = lax.all_gather(elemental, "space", axis=0, tiled=True)
    time_count = gathered.shape[0]
    sources = jnp.mod(sinks - tile_sep, time_count)

    def holder_block(items):
        tiles, sink_ids, source_ids, diagram = items
        return contract_tiles(gathered[sink_ids], gathered[source_ids], tiles, diagram)

    correlator = run_blocks(holder_block, (perambulator, sinks, sources, tile_diagram), tile_count)
    return (elemental, correlator)


def solution(mesh):
    return jax.shard_map(
        local,
        mesh=mesh,
        in_specs=(
            P("groups", "space", None, None, None),
            P("groups"),
            P(("groups", "space"), None, None, None),
            P(("groups", "space"), None),
            P(("groups", "space")),
            P(("groups", "space")),
        ),
        out_specs=(P(("groups", "space"), None, None, None), P(("groups", "space"), None)),
        check_vma=False,
    )
```

profile of v0, /device:TPU:0, one launch (start us, length us, event | category | flops | bytes accessed | tf_op | source)
XLA Modules:
  0.0 76.8 jit_solution(16801960626893713510)
XLA Ops:
  7.2 0.0 copy-start.2
  7.2 0.0 copy-start
  7.2 7.6 %all-to-all-start = ((bf16[16,4,2,3,128]{4,2,3,1,0:T(2,128)(2,1)}), bf16[16,4,2,3,128]{4,2,3,1,0:T(2,128)(2,1)S(1)}, u32[]{:S(2)}, u32[]{:S(2)}) async-start(bf16[16,4,2,3,128]{4,2,3,1,0:T(2,128)(2,1)} %param.6), calls=%async_computation | async-start | bytes 196608 | tf_op jit(solution)/shard_map/all_to_all | solution.py:65
  14.7 0.0 all-gather.3.cloned.1.call-start
  14.9 7.3 %all-to-all-done = bf16[16,4,2,3,128]{4,2,3,1,0:T(2,128)(2,1)S(1)} async-done(((bf16[16,4,2,3,128]{4,2,3,1,0:T(2,128)(2,1)}), bf16[16,4,2,3,128]{4,2,3,1,0:T(2,128)(2,1)S(1)}, u32[]{:S(2)}, u32[]{:S(2)}) %all-to-all-start) | async-done | bytes 98336 | tf_op jit(solution)/shard_map/all_to_all | solution.py:65
  22.2 0.1 fusion.15
  22.3 0.1 fusion.21
  22.4 0.3 fusion
  22.6 0.7 copy.37
  23.4 0.0 all-gather.3.cloned.1.call-update
  23.4 0.1 slice_bitcast_fusion.5
  23.5 0.3 copy.40
  23.8 0.0 copy-start.4
  23.8 0.3 copy.42
  24.1 0.4 copy-done.4
  24.5 0.6 copy-done.3
  25.1 0.0 copy-start.5
  25.2 0.6 copy-done.5
  25.8 0.7 copy.49
  26.5 32.4 %all-gather.3.cloned.1.call-done = bf16[32,128,128]{2,1,0:T(8,128)(2,1)} async-done(((bf16[2,128,128]{2,1,0:T(8,128)(2,1)}), bf16[32,128,128]{2,1,0:T(8,128)(2,1)}) %all-gather.3.cloned.1.call-update) | async-done | bytes 1048592 | tf_op jit(solution)/shard_map/all_gather | solution.py:70
  59.0 2.9 %gather_fusion.1 = bf16[16,2,128,128]{3,2,1,0:T(8,128)(2,1)} fusion(bf16[16,2,128,128]{3,2,1,0:T(8,128)(2,1)} %bitcast.124, s32[1024]{0:T(1024)S(1)} %pad_clamp_fusion), kind=kCustom, calls=%fused_computation.1 | custom fusion | bytes 2097216 | tf_op jit(solution)/shard_map/while/body/eval_jaxpr/gather | solution.py:76
  61.9 2.0 %gather_fusion = bf16[16,2,128,128]{3,2,1,0:T(8,128)(2,1)S(1)} fusion(bf16[16,2,128,128]{3,2,1,0:T(8,128)(2,1)} %bitcast.125, s32[1024]{0:T(1024)S(1)} %pad_clamp_fusion.1), kind=kCustom, calls=%fused_computation | custom fusion | bytes 2097216 | tf_op jit(solution)/shard_map/while/body/eval_jaxpr/gather | solution.py:76
  63.9 1.5 %fusion.5 = f32[16,128,128]{2,1,0:T(8,128)S(1)} fusion(bf16[16,2,128,128]{3,2,1,0:T(8,128)(2,1)} %gather_fusion.1, pred[16]{0:T(512)(128)(4,1)S(1)} %broadcast_compare_fusion, bf16[16,128,128]{1,2,0:T(8,128)(2,1)S(1)} %copy.42, bf16[16,2,128,128]{3,2,1,0:T(8,128)(2,1)S(1)} %copy-done), kind=kOutput, calls=%fused_computation.24 | convolution fusion | flops 67633152 | bytes 2621952 | tf_op jit(solution)/shard_map/while/body/eval_jaxpr/bij,bjk->bik/dot_general | solution.py:30
  65.4 0.4 fusion.3
  65.7 0.8 %copy-done.1 = bf16[16,2,128,128]{3,2,1,0:T(8,128)(2,1)S(1)} copy-done((bf16[16,2,128,128]{3,2,1,0:T(8,128)(2,1)S(1)}, bf16[16,2,128,128]{3,2,1,0:T(8,128)(2,1)}, u32[]{:S(2)}) %copy-start.1) | copy-done | bytes 1048600
  66.6 0.4 fusion.6
  67.0 0.4 fusion.4
  67.4 0.4 convolution_add_fusion
  67.8 0.4 convolution_subtract_fusion
  68.2 0.4 convolution_subtract_fusion.1
  68.6 0.7 subtract_reduce_fusion
  69.3 0.6 pad_maximum_fusion
  (12 shorter events, 0.1 us)
Async XLA Ops:
  7.2 7.6 %copy-start.2 = (s32[64]{0:T(128)S(1)}, s32[64]{0:T(128)}, u32[]{:S(2)}) copy-start(s32[64]{0:T(128)} %param.7) | copy-start | bytes 772
  7.2 16.3 %copy-start = (bf16[16,2,128,128]{3,2,1,0:T(8,128)(2,1)S(1)}, bf16[16,2,128,128]{3,2,1,0:T(8,128)(2,1)}, u32[]{:S(2)}) copy-start(bf16[16,2,128,128]{3,2,1,0:T(8,128)(2,1)} %param.8) | copy-start | bytes 3145732
  7.2 14.9 %all-to-all-start = ((bf16[16,4,2,3,128]{4,2,3,1,0:T(2,128)(2,1)}), bf16[16,4,2,3,128]{4,2,3,1,0:T(2,128)(2,1)S(1)}, u32[]{:S(2)}, u32[]{:S(2)}) async-start(bf16[16,4,2,3,128]{4,2,3,1,0:T(2,128)(2,1)} %param.6), calls=%async_computation | async-start | bytes 196608 | tf_op jit(solution)/shard_map/all_to_all | solution.py:65
  14.7 44.2 %all-gather.3.cloned.1.call-start = ((), (), s32[]{:S(2)}) async-start(), calls=%async_computation.1 | async-start | bytes 1114112 | tf_op jit(solution)/shard_map/all_gather | solution.py:70
  23.8 0.7 copy-start.4
  24.5 0.7 copy-start.3
  25.1 0.7 copy-start.5
  65.3 1.2 %copy-start.1 = (bf16[16,2,128,128]{3,2,1,0:T(8,128)(2,1)S(1)}, bf16[16,2,128,128]{3,2,1,0:T(8,128)(2,1)}, u32[]{:S(2)}) copy-start(bf16[16,2,128,128]{3,2,1,0:T(8,128)(2,1)} %gather_fusion.1) | copy-start | bytes 3145732
Sparse Core Ops, SparseCore 0:
  23.5 35.3 all-gather.2
where the time goes:
time: 77.1 us; the launch traced here: 76.8 us
  waiting for transfers between devices  39.7 us (51%)
  between operations  14.2 us (18%)
  local copies, waits for them, and re-layouts  9.55 us (12%)
  starting transfers between devices  7.6 us (10%)
  matrix products  4.81 us (6%)
  other arithmetic  0.85 us (1%)
    all_gather x1, waiting for transfers between devices, local(): gathered = lax.all_gather(elemental, 'space', axis=0, tiled=True)  32.4 us
    all_to_all x1, starting transfers between devices, local(): lax.all_to_all(eigvecs, 'space', split_axis=0, concat_axis=1, tiled=True)  7.56 us
    all_to_all x1, waiting for transfers between devices, local(): lax.all_to_all(eigvecs, 'space', split_axis=0, concat_axis=1, tiled=True)  7.27 us
    dot_general x8, matrix products, mult(): jnp.einsum('bij,bjk->bik', left, right, preferred_element_type=jnp.float32)  4.56 us
    unnamed x13, local copies, waits for them, and re-layouts  3.24 us
    gather x1, local copies, waits for them, and re-layouts, holder_block(): gathered[source_ids]  2.92 us
    gather x1, local copies, waits for them, and re-layouts, holder_block(): gathered[sink_ids]  1.97 us
  transfers between devices with their start and end apart: 2, of which 2 were waited for; matrix products, arithmetic and copies ran while one was open for 2% of the time, Pallas kernels for 0%

commit v1 on v0

--- a/solution.py
+++ b/solution.py
@@ -67,7 +67,24 @@
     right = make_right(vecs, cosine, sine)
     value = jnp.einsum("spck,spcol->okl", vecs, right, preferred_element_type=jnp.float32)
     elemental = value.astype(jnp.bfloat16)[None]
-    gathered = lax.all_gather(elemental, "space", axis=0, tiled=True)
+    ways, here, step = (lax.axis_size("space"), lax.axis_index("space"), elemental.shape[0])
+    shape = [n * ways if d == 0 else n for d, n in enumerate(elemental.shape)]
+    gathered = lax.dynamic_update_slice_in_dim(
+        jnp.zeros(shape, elemental.dtype), elemental, here * step, axis=0
+    )
+    going_up = going_down = elemental
+    for far in range(1, ways // 2 + 1):
+        going_up = lax.ppermute(going_up, "space", [(d, (d + 1) % ways) for d in range(ways)])
+        gathered = lax.dynamic_update_slice_in_dim(
+            gathered, going_up, (here - far) % ways * step, axis=0
+        )
+        if 2 * far < ways:
+            going_down = lax.ppermute(
+                going_down, "space", [(d, (d - 1) % ways) for d in range(ways)]
+            )
+            gathered = lax.dynamic_update_slice_in_dim(
+                gathered, going_down, (here + far) % ways * step, axis=0
+            )
     time_count = gathered.shape[0]
     sources = jnp.mod(sinks - tile_sep, time_count)
 

time: 77.1 us -> 81.7 us (1.060)
  between operations: 14.2 us -> 1.42 us
  waiting for transfers between devices: 39.7 us -> 50.7 us
  starting transfers between devices: 7.6 us -> 12.5 us
  local copies, waits for them, and re-layouts: 9.55 us -> 11.1 us
    ppermute x0 -> x15, waiting for transfers between devices: none -> 48.2 us  [the longest x8 48.2 us: local(): lax.ppermute(going_up, 'space', [(d, (d + 1) % ways) for d in range(ways)])]
    all_gather x1 -> x0, waiting for transfers between devices: 32.4 us -> none  [local(): gathered = lax.all_gather(elemental, 'space', axis=0, tiled=True)]
    ppermute x0 -> x15, starting transfers between devices: none -> 5.06 us  [the longest x8 3.04 us: local(): lax.ppermute(going_up, 'space', [(d, (d + 1) % ways) for d in range(ways)])]
    all_to_all x1, waiting for transfers between devices: 7.27 us -> 2.49 us  [local(): lax.all_to_all(eigvecs, 'space', split_axis=0, concat_axis=1, tiled=True)]
    ppermute x0 -> x15, local copies, waits for them, and re-layouts: none -> 1.78 us  [the longest x8 0.95 us: local(): lax.ppermute(going_up, 'space', [(d, (d + 1) % ways) for d in range(ways)])]
    gather x1, local copies, waits for them, and re-layouts: 2.92 us -> 1.67 us  [holder_block(): gathered[source_ids]]
    squeeze x2, local copies, waits for them, and re-layouts: 0.35 us -> 1.56 us  [contract_tiles(): tile_re = tiles[:, 0]]
    unnamed x13 -> x17, local copies, waits for them, and re-layouts: 3.24 us -> 3.57 us
  transfers between devices with their start and end apart: 2 -> 16, of which waited for: 2 -> 9; matrix products, arithmetic and copies ran while one was open for 2% -> 4% of each run, Pallas kernels for 0% -> 0%
where the time goes in v1:
time: 81.7 us; the launch traced here: 81.4 us
  waiting for transfers between devices  50.7 us (62%)
  starting transfers between devices  12.5 us (15%)
  local copies, waits for them, and re-layouts  11.1 us (14%)
  matrix products  4.9 us (6%)
  between operations  1.42 us (2%)
  other arithmetic  0.85 us (1%)
    ppermute x8, waiting for transfers between devices, local(): lax.ppermute(going_up, 'space', [(d, (d + 1) % ways) for d in range(ways)])  48.2 us
    all_to_all x1, starting transfers between devices, local(): lax.all_to_all(eigvecs, 'space', split_axis=0, concat_axis=1, tiled=True)  7.43 us
    dot_general x8, matrix products, mult(): jnp.einsum('bij,bjk->bik', left, right, preferred_element_type=jnp.float32)  4.64 us
    unnamed x17, local copies, waits for them, and re-layouts  3.57 us
    ppermute x8, starting transfers between devices, local(): lax.ppermute(going_up, 'space', [(d, (d + 1) % ways) for d in range(ways)])  3.04 us
    all_to_all x1, waiting for transfers between devices, local(): lax.all_to_all(eigvecs, 'space', split_axis=0, concat_axis=1, tiled=True)  2.49 us
    ppermute x7, starting transfers between devices, local(): lax.ppermute(going_down, 'space', [(d, (d - 1) % ways) for d in range(way...  2.02 us
    gather x1, local copies, waits for them, and re-layouts, holder_block(): gathered[source_ids]  1.67 us
  transfers between devices with their start and end apart: 16, of which 9 were waited for; matrix products, arithmetic and copies ran while one was open for 4% of the time, Pallas kernels for 0%

profile of v1, /device:TPU:0, one launch (start us, length us, event | category | flops | bytes accessed | tf_op | source)
XLA Modules:
  0.0 81.4 jit_solution(2651674202723037139)
XLA Ops:
  0.6 7.4 %all-to-all-start = ((bf16[16,4,2,3,128]{4,2,3,1,0:T(2,128)(2,1)}), bf16[16,4,2,3,128]{4,2,3,1,0:T(2,128)(2,1)S(1)}, u32[]{:S(2)}, u32[]{:S(2)}) async-start(bf16[16,4,2,3,128]{4,2,3,1,0:T(2,128)(2,1)} %param.6), calls=%async_computation | async-start | bytes 196608 | tf_op jit(solution)/shard_map/all_to_all | solution.py:65
  8.3 0.6 copy-done.5
  9.0 0.6 copy-done.4
  9.6 0.6 copy-done.6
  10.3 1.3 %slice_bitcast_fusion.5 = (bf16[16,128,128]{2,1,0:T(8,128)(2,1)S(1)}, bf16[16,128,128]{2,1,0:T(8,128)(2,1)S(1)}) fusion(bf16[16,2,128,128]{3,2,1,0:T(8,128)(2,1)} %param.8), kind=kLoop, calls=%fused_computation.22 | loop fusion | bytes 2097152 | tf_op jit(solution)/shard_map/while/body/eval_jaxpr/squeeze | solution.py:32
  12.3 0.6 copy-done.7
  13.0 2.5 %all-to-all-done = bf16[16,4,2,3,128]{4,2,3,1,0:T(2,128)(2,1)S(1)} async-done(((bf16[16,4,2,3,128]{4,2,3,1,0:T(2,128)(2,1)}), bf16[16,4,2,3,128]{4,2,3,1,0:T(2,128)(2,1)S(1)}, u32[]{:S(2)}, u32[]{:S(2)}) %all-to-all-start) | async-done | bytes 98336 | tf_op jit(solution)/shard_map/all_to_all | solution.py:65
  16.1 1.7 %collective-permute-start.1 = (bf16[1,2,128,128]{2,3,1,0:T(8,128)(2,1)S(1)}, bf16[1,2,128,128]{2,3,1,0:T(8,128)(2,1)S(1)}, u32[]{:S(2)}, u32[]{:S(2)}) collective-permute-start(bf16[1,2,128,128]{2,3,1,0:T(8,128)(2,1)S(1)} %fusion.1), channel_id=1, source_target_pairs={{0,15},{1,0},{2,1},{3,2},{4,3},{5,4},{6,5},{7,6},{8,7},{9,8},{10,9... | collective-permute-start | bytes 196616 | tf_op jit(solution)/shard_map/ppermute | solution.py:82
  18.1 6.2 %collective-permute-done = bf16[1,2,128,128]{2,3,1,0:T(8,128)(2,1)S(1)} collective-permute-done((bf16[1,2,128,128]{2,3,1,0:T(8,128)(2,1)S(1)}, bf16[1,2,128,128]{2,3,1,0:T(8,128)(2,1)S(1)}, u32[]{:S(2)}, u32[]{:S(2)}) %collective-permute-start) | collective-permute-done | bytes 65568 | tf_op jit(solution)/shard_map/ppermute | solution.py:77
  24.6 0.5 collective-permute-start.2
  25.1 6.0 %collective-permute-done.2 = bf16[1,2,128,128]{2,3,1,0:T(8,128)(2,1)S(1)} collective-permute-done((bf16[1,2,128,128]{2,3,1,0:T(8,128)(2,1)S(1)}, bf16[1,2,128,128]{2,3,1,0:T(8,128)(2,1)S(1)}, u32[]{:S(2)}, u32[]{:S(2)}) %collective-permute-start.2) | collective-permute-done | bytes 65568 | tf_op jit(solution)/shard_map/ppermute | solution.py:77
  31.4 0.5 collective-permute-start.4
  31.9 6.0 %collective-permute-done.4 = bf16[1,2,128,128]{2,3,1,0:T(8,128)(2,1)S(1)} collective-permute-done((bf16[1,2,128,128]{2,3,1,0:T(8,128)(2,1)S(1)}, bf16[1,2,128,128]{2,3,1,0:T(8,128)(2,1)S(1)}, u32[]{:S(2)}, u32[]{:S(2)}) %collective-permute-start.4) | collective-permute-done | bytes 65568 | tf_op jit(solution)/shard_map/ppermute | solution.py:77
  38.3 0.5 collective-permute-start.6
  38.8 6.0 %collective-permute-done.6 = bf16[1,2,128,128]{2,3,1,0:T(8,128)(2,1)S(1)} collective-permute-done((bf16[1,2,128,128]{2,3,1,0:T(8,128)(2,1)S(1)}, bf16[1,2,128,128]{2,3,1,0:T(8,128)(2,1)S(1)}, u32[]{:S(2)}, u32[]{:S(2)}) %collective-permute-start.6) | collective-permute-done | bytes 65568 | tf_op jit(solution)/shard_map/ppermute | solution.py:77
  45.1 0.5 collective-permute-start.8
  45.6 6.0 %collective-permute-done.8 = bf16[1,2,128,128]{2,3,1,0:T(8,128)(2,1)S(1)} collective-permute-done((bf16[1,2,128,128]{2,3,1,0:T(8,128)(2,1)S(1)}, bf16[1,2,128,128]{2,3,1,0:T(8,128)(2,1)S(1)}, u32[]{:S(2)}, u32[]{:S(2)}) %collective-permute-start.8) | collective-permute-done | bytes 65568 | tf_op jit(solution)/shard_map/ppermute | solution.py:77
  52.0 0.5 collective-permute-start.10
  52.5 6.0 %collective-permute-done.10 = bf16[1,2,128,128]{2,3,1,0:T(8,128)(2,1)S(1)} collective-permute-done((bf16[1,2,128,128]{2,3,1,0:T(8,128)(2,1)S(1)}, bf16[1,2,128,128]{2,3,1,0:T(8,128)(2,1)S(1)}, u32[]{:S(2)}, u32[]{:S(2)}) %collective-permute-start.10) | collective-permute-done | bytes 65568 | tf_op jit(solution)/shard_map/ppermute | solution.py:77
  58.8 0.5 collective-permute-start.12
  59.3 5.9 %collective-permute-done.12 = bf16[1,2,128,128]{2,3,1,0:T(8,128)(2,1)S(1)} collective-permute-done((bf16[1,2,128,128]{2,3,1,0:T(8,128)(2,1)S(1)}, bf16[1,2,128,128]{2,3,1,0:T(8,128)(2,1)S(1)}, u32[]{:S(2)}, u32[]{:S(2)}) %collective-permute-start.12) | collective-permute-done | bytes 65568 | tf_op jit(solution)/shard_map/ppermute | solution.py:77
  65.6 6.2 %collective-permute-done.14 = bf16[1,2,128,128]{2,3,1,0:T(8,128)(2,1)S(1)} collective-permute-done((bf16[1,2,128,128]{2,3,1,0:T(8,128)(2,1)S(1)}, bf16[1,2,128,128]{2,3,1,0:T(8,128)(2,1)S(1)}, u32[]{:S(2)}, u32[]{:S(2)}) %collective-permute-start.14) | collective-permute-done | bytes 65568 | tf_op jit(solution)/shard_map/ppermute | solution.py:77
  71.9 1.7 %gather_fusion.1 = bf16[16,2,128,128]{3,2,1,0:T(8,128)(2,1)} fusion(bf16[16,2,128,128]{3,2,1,0:T(8,128)(2,1)S(1)} %constant_dynamic-update-slice_fusion, s32[1024]{0:T(1024)S(1)} %pad_clamp_fusion), kind=kCustom, calls=%fused_computation.1 | custom fusion | bytes 2097216 | tf_op jit(solution)/shard_map/while/body/eval_jaxpr/gather | solution.py:93
  73.6 1.7 %gather_fusion = bf16[16,2,128,128]{3,2,1,0:T(8,128)(2,1)} fusion(bf16[16,2,128,128]{3,2,1,0:T(8,128)(2,1)S(1)} %constant_dynamic-update-slice_fusion, s32[1024]{0:T(1024)S(1)} %pad_clamp_fusion.1), kind=kCustom, calls=%fused_computation | custom fusion | bytes 2097216 | tf_op jit(solution)/shard_map/while/body/eval_jaxpr/gather | solution.py:93
  75.3 1.5 %fusion.6 = f32[16,128,128]{2,1,0:T(8,128)S(1)} fusion(bf16[16,2,128,128]{3,2,1,0:T(8,128)(2,1)} %gather_fusion.1, pred[16]{0:T(512)(128)(4,1)S(1)} %broadcast_compare_fusion, bf16[16,128,128]{1,2,0:T(8,128)(2,1)S(1)} %copy.42, bf16[16,2,128,128]{3,2,1,0:T(8,128)(2,1)S(1)} %copy-done), kind=kOutput, calls=%fused_computation.25 | convolution fusion | flops 67633152 | bytes 2621952 | tf_op jit(solution)/shard_map/while/body/eval_jaxpr/bij,bjk->bik/dot_general | solution.py:30
  77.2 0.8 %copy-done.2 = bf16[16,2,128,128]{3,2,1,0:T(8,128)(2,1)S(1)} copy-done((bf16[16,2,128,128]{3,2,1,0:T(8,128)(2,1)S(1)}, bf16[16,2,128,128]{3,2,1,0:T(8,128)(2,1)}, u32[]{:S(2)}) %copy-start.2) | copy-done | bytes 1048600
  78.1 0.4 fusion.7
  78.9 0.4 convolution_add_fusion
  79.3 0.4 convolution_subtract_fusion
  79.7 0.4 convolution_subtract_fusion.1
  80.1 0.7 subtract_reduce_fusion
  80.8 0.6 pad_maximum_fusion
  (74 shorter events, 4.7 us)
Async XLA Ops:
  0.6 14.8 %all-to-all-start = ((bf16[16,4,2,3,128]{4,2,3,1,0:T(2,128)(2,1)}), bf16[16,4,2,3,128]{4,2,3,1,0:T(2,128)(2,1)S(1)}, u32[]{:S(2)}, u32[]{:S(2)}) async-start(bf16[16,4,2,3,128]{4,2,3,1,0:T(2,128)(2,1)} %param.6), calls=%async_computation | async-start | bytes 196608 | tf_op jit(solution)/shard_map/all_to_all | solution.py:65
  8.3 0.7 copy-start.5
  9.0 0.7 copy-start.4
  9.6 0.7 copy-start.6
  12.3 0.7 copy-start.7
  16.1 1.9 %copy-start.3 = (bf16[1,2,128,128]{3,2,1,0:T(8,128)(2,1)}, bf16[1,2,128,128]{3,2,1,0:T(8,128)(2,1)S(1)}, u32[]{:S(2)}) copy-start(bf16[1,2,128,128]{3,2,1,0:T(8,128)(2,1)S(1)} %copy.49) | copy-start | bytes 196612
  16.1 8.3 %collective-permute-start.1 = (bf16[1,2,128,128]{2,3,1,0:T(8,128)(2,1)S(1)}, bf16[1,2,128,128]{2,3,1,0:T(8,128)(2,1)S(1)}, u32[]{:S(2)}, u32[]{:S(2)}) collective-permute-start(bf16[1,2,128,128]{2,3,1,0:T(8,128)(2,1)S(1)} %fusion.1), channel_id=1, source_target_pairs={{0,15},{1,0},{2,1},{3,2},{4,3},{5,4},{6,5},{7,6},{8,7},{9,8},{10,9... | collective-permute-start | bytes 196616 | tf_op jit(solution)/shard_map/ppermute | solution.py:82
  17.8 6.5 %collective-permute-start = (bf16[1,2,128,128]{2,3,1,0:T(8,128)(2,1)S(1)}, bf16[1,2,128,128]{2,3,1,0:T(8,128)(2,1)S(1)}, u32[]{:S(2)}, u32[]{:S(2)}) collective-permute-start(bf16[1,2,128,128]{2,3,1,0:T(8,128)(2,1)S(1)} %fusion.1), channel_id=1, source_target_pairs={{0,1},{1,2},{2,3},{3,4},{4,5},{5,6},{6,7},{7,8},{8,9},{9,10},{10,1... | collective-permute-start | bytes 196616 | tf_op jit(solution)/shard_map/ppermute | solution.py:77
  24.5 6.7 %collective-permute-start.3 = (bf16[1,2,128,128]{2,3,1,0:T(8,128)(2,1)S(1)}, bf16[1,2,128,128]{2,3,1,0:T(8,128)(2,1)S(1)}, u32[]{:S(2)}, u32[]{:S(2)}) collective-permute-start(bf16[1,2,128,128]{2,3,1,0:T(8,128)(2,1)S(1)} %collective-permute-done.1), channel_id=1, source_target_pairs={{0,15},{1,0},{2,1},{3,2},{4,3},{5,4},{6,5},{7,6},{8,7},{9,8},{10,9... | collective-permute-start | bytes 196616 | tf_op jit(solution)/shard_map/ppermute | solution.py:82
  24.6 6.5 %collective-permute-start.2 = (bf16[1,2,128,128]{2,3,1,0:T(8,128)(2,1)S(1)}, bf16[1,2,128,128]{2,3,1,0:T(8,128)(2,1)S(1)}, u32[]{:S(2)}, u32[]{:S(2)}) collective-permute-start(bf16[1,2,128,128]{2,3,1,0:T(8,128)(2,1)S(1)} %collective-permute-done), channel_id=1, source_target_pairs={{0,1},{1,2},{2,3},{3,4},{4,5},{5,6},{6,7},{7,8},{8,9},{9,10},{10,1... | collective-permute-start | bytes 196616 | tf_op jit(solution)/shard_map/ppermute | solution.py:77
  31.4 6.7 %collective-permute-start.5 = (bf16[1,2,128,128]{2,3,1,0:T(8,128)(2,1)S(1)}, bf16[1,2,128,128]{2,3,1,0:T(8,128)(2,1)S(1)}, u32[]{:S(2)}, u32[]{:S(2)}) collective-permute-start(bf16[1,2,128,128]{2,3,1,0:T(8,128)(2,1)S(1)} %collective-permute-done.3), channel_id=1, source_target_pairs={{0,15},{1,0},{2,1},{3,2},{4,3},{5,4},{6,5},{7,6},{8,7},{9,8},{10,9... | collective-permute-start | bytes 196616 | tf_op jit(solution)/shard_map/ppermute | solution.py:82
  31.4 6.5 %collective-permute-start.4 = (bf16[1,2,128,128]{2,3,1,0:T(8,128)(2,1)S(1)}, bf16[1,2,128,128]{2,3,1,0:T(8,128)(2,1)S(1)}, u32[]{:S(2)}, u32[]{:S(2)}) collective-permute-start(bf16[1,2,128,128]{2,3,1,0:T(8,128)(2,1)S(1)} %collective-permute-done.2), channel_id=1, source_target_pairs={{0,1},{1,2},{2,3},{3,4},{4,5},{5,6},{6,7},{7,8},{8,9},{9,10},{10,1... | collective-permute-start | bytes 196616 | tf_op jit(solution)/shard_map/ppermute | solution.py:77
  38.2 6.7 %collective-permute-start.7 = (bf16[1,2,128,128]{2,3,1,0:T(8,128)(2,1)S(1)}, bf16[1,2,128,128]{2,3,1,0:T(8,128)(2,1)S(1)}, u32[]{:S(2)}, u32[]{:S(2)}) collective-permute-start(bf16[1,2,128,128]{2,3,1,0:T(8,128)(2,1)S(1)} %collective-permute-done.5), channel_id=1, source_target_pairs={{0,15},{1,0},{2,1},{3,2},{4,3},{5,4},{6,5},{7,6},{8,7},{9,8},{10,9... | collective-permute-start | bytes 196616 | tf_op jit(solution)/shard_map/ppermute | solution.py:82
  38.3 6.5 %collective-permute-start.6 = (bf16[1,2,128,128]{2,3,1,0:T(8,128)(2,1)S(1)}, bf16[1,2,128,128]{2,3,1,0:T(8,128)(2,1)S(1)}, u32[]{:S(2)}, u32[]{:S(2)}) collective-permute-start(bf16[1,2,128,128]{2,3,1,0:T(8,128)(2,1)S(1)} %collective-permute-done.4), channel_id=1, source_target_pairs={{0,1},{1,2},{2,3},{3,4},{4,5},{5,6},{6,7},{7,8},{8,9},{9,10},{10,1... | collective-permute-start | bytes 196616 | tf_op jit(solution)/shard_map/ppermute | solution.py:77
  45.0 6.7 %collective-permute-start.9 = (bf16[1,2,128,128]{2,3,1,0:T(8,128)(2,1)S(1)}, bf16[1,2,128,128]{2,3,1,0:T(8,128)(2,1)S(1)}, u32[]{:S(2)}, u32[]{:S(2)}) collective-permute-start(bf16[1,2,128,128]{2,3,1,0:T(8,128)(2,1)S(1)} %collective-permute-done.7), channel_id=1, source_target_pairs={{0,15},{1,0},{2,1},{3,2},{4,3},{5,4},{6,5},{7,6},{8,7},{9,8},{10,9... | collective-permute-start | bytes 196616 | tf_op jit(solution)/shard_map/ppermute | solution.py:82
  45.1 6.5 %collective-permute-start.8 = (bf16[1,2,128,128]{2,3,1,0:T(8,128)(2,1)S(1)}, bf16[1,2,128,128]{2,3,1,0:T(8,128)(2,1)S(1)}, u32[]{:S(2)}, u32[]{:S(2)}) collective-permute-start(bf16[1,2,128,128]{2,3,1,0:T(8,128)(2,1)S(1)} %collective-permute-done.6), channel_id=1, source_target_pairs={{0,1},{1,2},{2,3},{3,4},{4,5},{5,6},{6,7},{7,8},{8,9},{9,10},{10,1... | collective-permute-start | bytes 196616 | tf_op jit(solution)/shard_map/ppermute | solution.py:77
  51.9 6.7 %collective-permute-start.11 = (bf16[1,2,128,128]{2,3,1,0:T(8,128)(2,1)S(1)}, bf16[1,2,128,128]{2,3,1,0:T(8,128)(2,1)S(1)}, u32[]{:S(2)}, u32[]{:S(2)}) collective-permute-start(bf16[1,2,128,128]{2,3,1,0:T(8,128)(2,1)S(1)} %collective-permute-done.9), channel_id=1, source_target_pairs={{0,15},{1,0},{2,1},{3,2},{4,3},{5,4},{6,5},{7,6},{8,7},{9,8},{10,9... | collective-permute-start | bytes 196616 | tf_op jit(solution)/shard_map/ppermute | solution.py:82
  52.0 6.5 %collective-permute-start.10 = (bf16[1,2,128,128]{2,3,1,0:T(8,128)(2,1)S(1)}, bf16[1,2,128,128]{2,3,1,0:T(8,128)(2,1)S(1)}, u32[]{:S(2)}, u32[]{:S(2)}) collective-permute-start(bf16[1,2,128,128]{2,3,1,0:T(8,128)(2,1)S(1)} %collective-permute-done.8), channel_id=1, source_target_pairs={{0,1},{1,2},{2,3},{3,4},{4,5},{5,6},{6,7},{7,8},{8,9},{9,10},{10,1... | collective-permute-start | bytes 196616 | tf_op jit(solution)/shard_map/ppermute | solution.py:77
  58.7 6.7 %collective-permute-start.13 = (bf16[1,2,128,128]{2,3,1,0:T(8,128)(2,1)S(1)}, bf16[1,2,128,128]{2,3,1,0:T(8,128)(2,1)S(1)}, u32[]{:S(2)}, u32[]{:S(2)}) collective-permute-start(bf16[1,2,128,128]{2,3,1,0:T(8,128)(2,1)S(1)} %collective-permute-done.11), channel_id=1, source_target_pairs={{0,15},{1,0},{2,1},{3,2},{4,3},{5,4},{6,5},{7,6},{8,7},{9,8},{10,9... | collective-permute-start | bytes 196616 | tf_op jit(solution)/shard_map/ppermute | solution.py:82
  58.8 6.4 %collective-permute-start.12 = (bf16[1,2,128,128]{2,3,1,0:T(8,128)(2,1)S(1)}, bf16[1,2,128,128]{2,3,1,0:T(8,128)(2,1)S(1)}, u32[]{:S(2)}, u32[]{:S(2)}) collective-permute-start(bf16[1,2,128,128]{2,3,1,0:T(8,128)(2,1)S(1)} %collective-permute-done.10), channel_id=1, source_target_pairs={{0,1},{1,2},{2,3},{3,4},{4,5},{5,6},{6,7},{7,8},{8,9},{9,10},{10,1... | collective-permute-start | bytes 196616 | tf_op jit(solution)/shard_map/ppermute | solution.py:77
  65.4 6.4 %collective-permute-start.14 = (bf16[1,2,128,128]{2,3,1,0:T(8,128)(2,1)S(1)}, bf16[1,2,128,128]{2,3,1,0:T(8,128)(2,1)S(1)}, u32[]{:S(2)}, u32[]{:S(2)}) collective-permute-start(bf16[1,2,128,128]{2,3,1,0:T(8,128)(2,1)S(1)} %collective-permute-done.12), channel_id=1, source_target_pairs={{0,1},{1,2},{2,3},{3,4},{4,5},{5,6},{6,7},{7,8},{8,9},{9,10},{10,1... | collective-permute-start | bytes 196616 | tf_op jit(solution)/shard_map/ppermute | solution.py:77
  73.6 1.7 %copy-start = (bf16[16,2,128,128]{3,2,1,0:T(8,128)(2,1)S(1)}, bf16[16,2,128,128]{3,2,1,0:T(8,128)(2,1)}, u32[]{:S(2)}) copy-start(bf16[16,2,128,128]{3,2,1,0:T(8,128)(2,1)} %param.8) | copy-start | bytes 3145732
  75.3 1.6 %copy-start.1 = (bf16[16,2,128,128]{3,2,1,0:T(8,128)(2,1)S(1)}, bf16[16,2,128,128]{3,2,1,0:T(8,128)(2,1)}, u32[]{:S(2)}) copy-start(bf16[16,2,128,128]{3,2,1,0:T(8,128)(2,1)} %gather_fusion) | copy-start | bytes 3145732
  76.8 1.2 %copy-start.2 = (bf16[16,2,128,128]{3,2,1,0:T(8,128)(2,1)S(1)}, bf16[16,2,128,128]{3,2,1,0:T(8,128)(2,1)}, u32[]{:S(2)}) copy-start(bf16[16,2,128,128]{3,2,1,0:T(8,128)(2,1)} %gather_fusion.1) | copy-start | bytes 3145732
